TPU v7x, 32 devices: a whole 2x2x4 slice. The times are simulated.
32 devices in a mesh: fsdp: 8 (over y, x, core), seq: 4 (over z).
Axes of the slice: x: 2, y: 2, z: 4, core: 2. Of those that a mesh axis runs over, the one named last changes fastest.
Arguments:
- hidden_in: bfloat16 [8, 1024, 1024], P('fsdp', 'seq'), may hold values from -6 to 6
- cotangent: float32 [8, 1024, 1024], P('fsdp', 'seq'), may hold values from -6 to 6
- doc_ids: int32 [8, 1024], P('fsdp'), may hold values from 0 to 3, never falling along the last dimension, each value on 1 to 512 neighbouring positions
- routes: int32 [8, 1024, 8], P('fsdp', 'seq'), may hold values from 0 to 31, all different within a row; in each aligned block of 256 rows (0 to 255, 256 to 511, ..., all dimensions but the last counted through in order) at most 96 rows name the same one
- gain_attn: bfloat16 [1024], P(('fsdp', 'seq')), may hold values from 0.5 to 1.5
- w_query: bfloat16 [1024, 1024], P(('fsdp', 'seq')), may hold values from -0.1875 to 0.1875
- w_key: bfloat16 [1024, 512], P(('fsdp', 'seq')), may hold values from -0.1875 to 0.1875
- w_value: bfloat16 [1024, 512], P(('fsdp', 'seq')), may hold values from -0.1875 to 0.1875
- w_out: bfloat16 [1024, 1024], P(('fsdp', 'seq')), may hold values from -5 to 5
- gain_ffn: bfloat16 [1024], P(('fsdp', 'seq')), may hold values from 0.5 to 1.5
- w_router: bfloat16 [1024, 32], P(('fsdp', 'seq')), may hold values from -0.1875 to 0.1875
- w_gate: bfloat16 [32, 1024, 512], P('fsdp', 'seq'), may hold values from -0.1875 to 0.1875
- w_up: bfloat16 [32, 1024, 512], P('fsdp', 'seq'), may hold values from -0.1875 to 0.1875
- w_down: bfloat16 [32, 512, 1024], P('fsdp', None, 'seq'), may hold values from -3 to 3
Outputs:
- output: float32 [8, 1024, 1024], P('fsdp', 'seq')
- d_input: float32 [8, 1024, 1024], P('fsdp', 'seq')
- grad_gain_attn: float32 [1024], P(('fsdp', 'seq'))
- grad_query: float32 [1024, 1024], P(('fsdp', 'seq'))
- grad_key: float32 [1024, 512], P(('fsdp', 'seq'))
- grad_value: float32 [1024, 512], P(('fsdp', 'seq'))
- grad_out: float32 [1024, 1024], P(('fsdp', 'seq'))
- grad_gain_ffn: float32 [1024], P(('fsdp', 'seq'))
- grad_router: float32 [1024, 32], P(('fsdp', 'seq'))
- grad_gate: float32 [32, 1024, 512], P('fsdp', 'seq')
- grad_up: float32 [32, 1024, 512], P('fsdp', 'seq')
- grad_down: float32 [32, 512, 1024], P('fsdp', None, 'seq')
Inputs may be any that keep to these rules, and one draw needn't show every extreme that they name: `doc_ids`: document numbers never fall along a sequence; a document spans 1 to 512 positions, one exactly 512. `routes`: the 8 experts of a token differ; among the tokens of one device no expert is named more than 96 times, a bound that some block reaches.
All inputs are finite; a program needn't handle non-finite values.
Results may differ from a plain program's by a relative error of at most 0.015.
Values may be sent and summed in bfloat16 or wider, within the bound.
A program may use at most 256 MiB of HBM per device.

v0:
```python
import jax
import jax.numpy as jnp
from jax import lax
from jax.sharding import PartitionSpec as P

HD = 64


EPS = 1e-06
ATTN_MULT = 0.015625
RESID_MULT = 0.22
THETA = 10000.0
NEG_FILL = -1e30


def rope_tables(positions, head_dim):
    half_dim = head_dim // 2
    frequency = THETA ** (-(jnp.arange(half_dim, dtype=jnp.float32) * 2.0 / head_dim))
    phases = positions.astype(jnp.float32)[:, None] * frequency[None, :]
    return (jnp.cos(phases), jnp.sin(phases))


def rotate(values, cosine, sine_tab):
    half_dim = values.shape[-1] // 2
    first_half = values[..., :half_dim]
    second_half = values[..., half_dim:]
    cos_b = cosine[:, None, :]
    sin_b = sine_tab[:, None, :]
    return jnp.concatenate(
        [first_half * cos_b - second_half * sin_b, second_half * cos_b + first_half * sin_b],
        axis=-1,
    )


def unrotate(grad_vals, cosine, sine_tab):
    half_dim = grad_vals.shape[-1] // 2
    first_half = grad_vals[..., :half_dim]
    second_half = grad_vals[..., half_dim:]
    cos_b = cosine[:, None, :]
    sin_b = sine_tab[:, None, :]
    return jnp.concatenate(
        [first_half * cos_b + second_half * sin_b, second_half * cos_b - first_half * sin_b],
        axis=-1,
    )


def rms_scale(values):
    return lax.rsqrt(jnp.mean(values * values, axis=-1, keepdims=True) + EPS)


def norm_backward(inputs, scale, gain, d_normed):
    upstream = gain * d_normed
    d_inputs = scale * upstream - inputs * scale**3 * jnp.mean(
        upstream * inputs, axis=-1, keepdims=True
    )
    d_gain = jnp.sum(d_normed * inputs * scale, axis=0)
    return (d_inputs, d_gain)


def expert_forward(inbound, gathered_gate, gathered_up, gathered_down):
    pre_gate = jnp.einsum(
        "secd,edf->secf", inbound, gathered_gate, preferred_element_type=jnp.float32
    )
    pre_up = jnp.einsum("secd,edf->secf", inbound, gathered_up, preferred_element_type=jnp.float32)
    sigm = jax.nn.sigmoid(pre_gate)
    act = (pre_gate * sigm * pre_up).astype(jnp.bfloat16)
    expert_out = jnp.einsum(
        "secf,efd->secd", act, gathered_down, preferred_element_type=jnp.float32
    ).astype(jnp.bfloat16)
    return (pre_gate, pre_up, sigm, act, expert_out)


def expert_backward(
    inbound, d_inbound, pre_gate, pre_up, sigm, act, gathered_gate, gathered_up, gathered_down
):
    d_act = jnp.einsum(
        "secd,efd->secf", d_inbound, gathered_down, preferred_element_type=jnp.float32
    )
    grad_down = jnp.einsum("secf,secd->efd", act, d_inbound, preferred_element_type=jnp.float32)
    d_up = (d_act * pre_gate * sigm).astype(jnp.bfloat16)
    d_pre_gate = (d_act * pre_up * sigm * (1.0 + pre_gate * (1.0 - sigm))).astype(jnp.bfloat16)
    grad_gate = jnp.einsum(
        "secd,secf->edf", inbound, d_pre_gate, preferred_element_type=jnp.float32
    )
    grad_up = jnp.einsum("secd,secf->edf", inbound, d_up, preferred_element_type=jnp.float32)
    d_inputs = (
        jnp.einsum("secf,edf->secd", d_pre_gate, gathered_gate, preferred_element_type=jnp.float32)
        + jnp.einsum("secf,edf->secd", d_up, gathered_up, preferred_element_type=jnp.float32)
    ).astype(jnp.bfloat16)
    return (grad_gate, grad_up, grad_down, d_inputs)


def on_device(
    hidden_in,
    cotangent,
    doc_ids,
    routes,
    gain_attn,
    w_query,
    w_key,
    w_value,
    w_out,
    gain_ffn,
    w_router,
    w_gate,
    w_up,
    w_down,
):
    n_seq = lax.axis_size("seq")
    n_fsdp = lax.axis_size("fsdp")
    tok_rows = hidden_in.shape[1]
    width = hidden_in.shape[2]
    seq_len = tok_rows * n_seq
    top_k = routes.shape[2]
    n_expert = w_router.shape[1]
    local_exp = w_gate.shape[0]
    head_dim = HD
    q_width = w_query.shape[1]
    kv_width = w_key.shape[1]
    heads_here = q_width // head_dim // n_seq
    kv_here = kv_width // head_dim // n_seq
    group_size = heads_here // kv_here
    slot_cap = 3 * tok_rows * top_k // (2 * n_expert)
    n_slots = n_expert * slot_cap
    full_gain_attn, full_query, full_key, full_value, full_out, full_gain_ffn, full_router = (
        lax.all_gather(gain_attn, ("fsdp", "seq"), axis=0, tiled=True),
        lax.all_gather(w_query, ("fsdp", "seq"), axis=0, tiled=True),
        lax.all_gather(w_key, ("fsdp", "seq"), axis=0, tiled=True),
        lax.all_gather(w_value, ("fsdp", "seq"), axis=0, tiled=True),
        lax.all_gather(w_out, ("fsdp", "seq"), axis=0, tiled=True),
        lax.all_gather(gain_ffn, ("fsdp", "seq"), axis=0, tiled=True),
        lax.all_gather(w_router, ("fsdp", "seq"), axis=0, tiled=True),
    )
    gain_one = full_gain_attn.astype(jnp.float32)
    gain_two = full_gain_ffn.astype(jnp.float32)
    tokens = hidden_in[0].astype(jnp.float32)
    scale_one = rms_scale(tokens)
    normed_one = (tokens * scale_one * gain_one).astype(jnp.bfloat16)
    tok_pos = lax.axis_index("seq") * tok_rows + jnp.arange(tok_rows, dtype=jnp.int32)
    cos_tok, sin_tok = rope_tables(tok_pos, head_dim)
    query = jnp.dot(normed_one, full_query, preferred_element_type=jnp.float32).reshape(
        tok_rows, -1, head_dim
    )
    keys_tok = jnp.dot(normed_one, full_key, preferred_element_type=jnp.float32).reshape(
        tok_rows, -1, head_dim
    )
    query = (
        rotate(query, cos_tok, sin_tok)
        .astype(jnp.bfloat16)
        .reshape(tok_rows, n_seq, heads_here * head_dim)
    )
    keys_tok = (
        rotate(keys_tok, cos_tok, sin_tok)
        .astype(jnp.bfloat16)
        .reshape(tok_rows, n_seq, kv_here * head_dim)
    )
    values_tok = jnp.dot(normed_one, full_value, preferred_element_type=jnp.float32).astype(
        jnp.bfloat16
    )
    key_value = jnp.concatenate(
        [keys_tok, values_tok.reshape(tok_rows, n_seq, kv_here * head_dim)], axis=-1
    )
    q_recv, kv_recv = (
        lax.all_to_all(query, "seq", split_axis=1, concat_axis=0, tiled=True),
        lax.all_to_all(key_value, "seq", split_axis=1, concat_axis=0, tiled=True),
    )
    q_heads = q_recv.reshape(seq_len, kv_here, group_size, head_dim)
    k_heads = kv_recv[:, 0, : kv_here * head_dim].reshape(seq_len, kv_here, head_dim)
    v_heads = kv_recv[:, 0, kv_here * head_dim :].reshape(seq_len, kv_here, head_dim)
    doc_row = doc_ids[0]
    key_pos = jnp.arange(seq_len, dtype=jnp.int32)
    block_rows = min(512, seq_len)
    starts = list(range(0, seq_len, block_rows))

    def block_scores(row_start):
        q_blk = q_heads[row_start : row_start + block_rows]
        query_pos = row_start + jnp.arange(block_rows, dtype=jnp.int32)
        allowed = (query_pos[:, None] >= key_pos[None, :]) & (
            doc_row[row_start : row_start + block_rows][:, None] == doc_row[None, :]
        )
        scores = (
            jnp.einsum("qkgd,skd->kgqs", q_blk, k_heads, preferred_element_type=jnp.float32)
            * ATTN_MULT
        )
        return (q_blk, jnp.where(allowed[None, None], scores, NEG_FILL))

    attn_parts = []
    lse_parts = []
    for row_start in starts:
        q_blk, scores = block_scores(row_start)
        top_val = jnp.max(scores, axis=-1, keepdims=True)
        expo_vals = jnp.exp(scores - top_val)
        row_total = jnp.sum(expo_vals, axis=-1, keepdims=True)
        lse_parts.append(top_val[..., 0] + jnp.log(row_total[..., 0]))
        prob_vals = (expo_vals / row_total).astype(jnp.bfloat16)
        attn_parts.append(
            jnp.einsum(
                "kgqs,skd->qkgd", prob_vals, v_heads, preferred_element_type=jnp.float32
            ).astype(jnp.bfloat16)
        )
    attn_heads = jnp.concatenate(attn_parts, axis=0)
    log_total = jnp.concatenate(lse_parts, axis=2)
    attn_tok = lax.all_to_all(
        attn_heads.reshape(seq_len, 1, heads_here * head_dim),
        "seq",
        split_axis=0,
        concat_axis=1,
        tiled=True,
    ).reshape(tok_rows, q_width)
    branch = jnp.dot(attn_tok, full_out, preferred_element_type=jnp.float32)
    resid = tokens + RESID_MULT * branch
    scale_two = rms_scale(resid)
    normed_two = (resid * scale_two * gain_two).astype(jnp.bfloat16)
    logits = jnp.dot(normed_two, full_router, preferred_element_type=jnp.float32)
    route_row = routes[0]
    onehot = route_row[:, :, None] == jnp.arange(n_expert, dtype=jnp.int32)[None, None, :]
    chosen = jnp.sum(jnp.where(onehot, logits[:, None, :], 0.0), axis=-1)
    top_val = jnp.max(chosen, axis=-1, keepdims=True)
    expo_vals = jnp.exp(chosen - top_val)
    gates = expo_vals / jnp.sum(expo_vals, axis=-1, keepdims=True)
    hits = onehot.reshape(tok_rows * top_k, n_expert).astype(jnp.int32)
    before = jnp.cumsum(hits, axis=0, dtype=jnp.int32) - hits
    place = jnp.sum(before * hits, axis=1, dtype=jnp.int32)
    slot_of = route_row.reshape(-1) * slot_cap + place
    token_of = jnp.arange(tok_rows * top_k, dtype=jnp.int32) // top_k
    slot_token = jnp.zeros((n_slots,), jnp.int32).at[slot_of].set(token_of)
    slot_live = (
        jnp.zeros((n_slots,), jnp.bfloat16)
        .at[slot_of]
        .set(jnp.ones((tok_rows * top_k,), jnp.bfloat16))
    )
    slot_gate = jnp.zeros((n_slots,), jnp.float32).at[slot_of].set(gates.reshape(-1))
    grad_in = cotangent[0]
    d_moe = RESID_MULT * grad_in
    gathered_gate, gathered_up, gathered_down = (
        lax.all_gather(w_gate, "seq", axis=1, tiled=True),
        lax.all_gather(w_up, "seq", axis=1, tiled=True),
        lax.all_gather(w_down, "seq", axis=2, tiled=True),
    )
    outbound = (jnp.take(normed_two, slot_token, axis=0) * slot_live[:, None]).reshape(
        n_fsdp, local_exp * slot_cap, width
    )
    inbound = lax.all_to_all(outbound, "fsdp", split_axis=0, concat_axis=0, tiled=True).reshape(
        n_fsdp, local_exp, slot_cap, width
    )
    pre_gate, pre_up, sigm, act, expert_out = expert_forward(
        inbound, gathered_gate, gathered_up, gathered_down
    )
    returned = lax.all_to_all(
        expert_out.reshape(n_fsdp, local_exp * slot_cap, width),
        "fsdp",
        split_axis=0,
        concat_axis=0,
        tiled=True,
    ).reshape(n_slots, width)
    d_slot = (slot_gate[:, None] * jnp.take(d_moe, slot_token, axis=0)).astype(jnp.bfloat16)
    d_inbound = lax.all_to_all(
        d_slot.reshape(n_fsdp, local_exp * slot_cap, width),
        "fsdp",
        split_axis=0,
        concat_axis=0,
        tiled=True,
    ).reshape(n_fsdp, local_exp, slot_cap, width)
    grad_gate, grad_up, grad_down, d_inputs = expert_backward(
        inbound, d_inbound, pre_gate, pre_up, sigm, act, gathered_gate, gathered_up, gathered_down
    )
    d_back = lax.all_to_all(
        d_inputs.reshape(n_fsdp, local_exp * slot_cap, width),
        "fsdp",
        split_axis=0,
        concat_axis=0,
        tiled=True,
    ).reshape(n_slots, width)
    picked = jnp.take(returned, slot_of, axis=0).reshape(tok_rows, top_k, width).astype(jnp.float32)
    moe = jnp.sum(gates[:, :, None] * picked, axis=1)
    output = resid + RESID_MULT * moe
    d_gates = jnp.sum(d_moe[:, None, :] * picked, axis=-1)
    owned_gate, owned_up, owned_down = (
        lax.psum_scatter(
            grad_gate.astype(jnp.bfloat16), "seq", scatter_dimension=1, tiled=True
        ).astype(jnp.float32),
        lax.psum_scatter(
            grad_up.astype(jnp.bfloat16), "seq", scatter_dimension=1, tiled=True
        ).astype(jnp.float32),
        lax.psum_scatter(
            grad_down.astype(jnp.bfloat16), "seq", scatter_dimension=2, tiled=True
        ).astype(jnp.float32),
    )
    d_from_experts = jnp.sum(
        jnp.take(d_back, slot_of, axis=0).reshape(tok_rows, top_k, width).astype(jnp.float32),
        axis=1,
    )
    d_chosen = gates * (d_gates - jnp.sum(gates * d_gates, axis=-1, keepdims=True))
    d_logits = jnp.sum(jnp.where(onehot, d_chosen[:, :, None], 0.0), axis=1).astype(jnp.bfloat16)
    d_normed_two = d_from_experts + jnp.einsum(
        "te,de->td", d_logits, full_router, preferred_element_type=jnp.float32
    )
    grad_router = jnp.einsum("td,te->de", normed_two, d_logits, preferred_element_type=jnp.float32)
    d_norm_two, grad_gain_two = norm_backward(resid, scale_two, gain_two, d_normed_two)
    d_resid = grad_in + d_norm_two
    d_branch = (RESID_MULT * d_resid).astype(jnp.bfloat16)
    grad_out = jnp.einsum("tq,td->qd", attn_tok, d_branch, preferred_element_type=jnp.float32)
    d_attn = jnp.einsum("td,qd->tq", d_branch, full_out, preferred_element_type=jnp.float32).astype(
        jnp.bfloat16
    )
    d_heads = lax.all_to_all(
        d_attn.reshape(tok_rows, n_seq, heads_here * head_dim),
        "seq",
        split_axis=1,
        concat_axis=0,
        tiled=True,
    ).reshape(seq_len, kv_here, group_size, head_dim)
    d_query_parts = []
    d_key_sum = jnp.zeros((seq_len, kv_here, head_dim), jnp.float32)
    d_val_sum = jnp.zeros((seq_len, kv_here, head_dim), jnp.float32)
    for row_start in starts:
        q_blk, scores = block_scores(row_start)
        lse_blk = log_total[:, :, row_start : row_start + block_rows]
        prob_vals = jnp.exp(scores - lse_blk[..., None])
        d_out_blk = d_heads[row_start : row_start + block_rows]
        attn_blk = attn_heads[row_start : row_start + block_rows]
        d_val_sum = d_val_sum + jnp.einsum(
            "kgqs,qkgd->skd",
            prob_vals.astype(jnp.bfloat16),
            d_out_blk,
            preferred_element_type=jnp.float32,
        )
        d_prob = jnp.einsum(
            "qkgd,skd->kgqs", d_out_blk, v_heads, preferred_element_type=jnp.float32
        )
        row_delta = jnp.transpose(
            jnp.sum(d_out_blk.astype(jnp.float32) * attn_blk.astype(jnp.float32), axis=-1),
            (1, 2, 0),
        )
        d_score = (prob_vals * (d_prob - row_delta[..., None]) * ATTN_MULT).astype(jnp.bfloat16)
        d_query_parts.append(
            jnp.einsum("kgqs,skd->qkgd", d_score, k_heads, preferred_element_type=jnp.float32)
        )
        d_key_sum = d_key_sum + jnp.einsum(
            "kgqs,qkgd->skd", d_score, q_blk, preferred_element_type=jnp.float32
        )
    cos_full, sin_full = rope_tables(key_pos, head_dim)
    d_query_all = jnp.concatenate(d_query_parts, axis=0).reshape(seq_len, heads_here, head_dim)
    d_query_rot = (
        unrotate(d_query_all, cos_full, sin_full)
        .astype(jnp.bfloat16)
        .reshape(seq_len, 1, heads_here * head_dim)
    )
    d_key_rot = (
        unrotate(d_key_sum, cos_full, sin_full)
        .astype(jnp.bfloat16)
        .reshape(seq_len, 1, kv_here * head_dim)
    )
    d_val_low = d_val_sum.astype(jnp.bfloat16).reshape(seq_len, 1, kv_here * head_dim)
    d_kv = jnp.concatenate([d_key_rot, d_val_low], axis=-1)
    d_query_tok, d_kv_tok = (
        lax.all_to_all(d_query_rot, "seq", split_axis=0, concat_axis=1, tiled=True),
        lax.all_to_all(d_kv, "seq", split_axis=0, concat_axis=1, tiled=True),
    )
    d_query_tok = d_query_tok.reshape(tok_rows, q_width)
    d_key_tok = d_kv_tok[:, :, : kv_here * head_dim].reshape(tok_rows, kv_width)
    d_val_tok = d_kv_tok[:, :, kv_here * head_dim :].reshape(tok_rows, kv_width)
    d_normed_one = (
        jnp.einsum("tq,dq->td", d_query_tok, full_query, preferred_element_type=jnp.float32)
        + jnp.einsum("tk,dk->td", d_key_tok, full_key, preferred_element_type=jnp.float32)
        + jnp.einsum("tk,dk->td", d_val_tok, full_value, preferred_element_type=jnp.float32)
    )
    grad_query = jnp.einsum(
        "td,tq->dq", normed_one, d_query_tok, preferred_element_type=jnp.float32
    )
    grad_key = jnp.einsum("td,tk->dk", normed_one, d_key_tok, preferred_element_type=jnp.float32)
    grad_value = jnp.einsum("td,tk->dk", normed_one, d_val_tok, preferred_element_type=jnp.float32)
    d_norm_one, grad_gain_one = norm_backward(tokens, scale_one, gain_one, d_normed_one)
    d_input = d_resid + d_norm_one
    own_gain_one, own_query, own_key, own_value, own_out, own_gain_two, own_router = (
        lax.psum_scatter(grad_gain_one, ("fsdp", "seq"), scatter_dimension=0, tiled=True),
        lax.psum_scatter(grad_query, ("fsdp", "seq"), scatter_dimension=0, tiled=True),
        lax.psum_scatter(grad_key, ("fsdp", "seq"), scatter_dimension=0, tiled=True),
        lax.psum_scatter(grad_value, ("fsdp", "seq"), scatter_dimension=0, tiled=True),
        lax.psum_scatter(grad_out, ("fsdp", "seq"), scatter_dimension=0, tiled=True),
        lax.psum_scatter(grad_gain_two, ("fsdp", "seq"), scatter_dimension=0, tiled=True),
        lax.psum_scatter(grad_router, ("fsdp", "seq"), scatter_dimension=0, tiled=True),
    )
    return (
        output[None],
        d_input[None],
        own_gain_one,
        own_query,
        own_key,
        own_value,
        own_out,
        own_gain_two,
        own_router,
        owned_gate,
        owned_up,
        owned_down,
    )


def solution(mesh):
    placed = (
        P("fsdp", "seq", None),
        P("fsdp", "seq", None),
        P("fsdp", None),
        P("fsdp", "seq", None),
        P(("fsdp", "seq")),
        P(("fsdp", "seq"), None),
        P(("fsdp", "seq"), None),
        P(("fsdp", "seq"), None),
        P(("fsdp", "seq"), None),
        P(("fsdp", "seq")),
        P(("fsdp", "seq"), None),
        P("fsdp", "seq", None),
        P("fsdp", "seq", None),
        P("fsdp", None, "seq"),
    )
    return jax.shard_map(
        on_device,
        mesh=mesh,
        in_specs=placed,
        out_specs=(
            P("fsdp", "seq", None),
            P("fsdp", "seq", None),
            P(("fsdp", "seq")),
            P(("fsdp", "seq"), None),
            P(("fsdp", "seq"), None),
            P(("fsdp", "seq"), None),
            P(("fsdp", "seq"), None),
            P(("fsdp", "seq")),
            P(("fsdp", "seq"), None),
            P("fsdp", "seq", None),
            P("fsdp", "seq", None),
            P("fsdp", None, "seq"),
        ),
        check_vma=False,
    )
```

profile of v0, /device:TPU:0, one launch (start us, length us, event | category | flops | bytes accessed | tf_op | source)
XLA Modules:
  0.0 1681.3 jit_solution(14716712160179753947)
XLA Ops:
  16.4 42.0 %all-reduce.5 = (bf16[1024]{0:T(1024)(128)(2,1)S(1)}, bf16[1024]{0:T(1024)(128)(2,1)S(1)}) all-reduce(bf16[1024]{0:T(1024)(128)(2,1)S(1)} %dynamic-update-slice, bf16[1024]{0:T(1024)(128)(2,1)S(1)} %dynamic-update-slice.1), channel_id=1, replica_groups=mesh['fsdp'=8,'seq'=4] {'fsdp','seq'}, use_global_device_ids=true, to_apply=%add | all-reduce | flops 2048 | bytes 8192
  58.8 9.1 reduce-window.6
  70.8 52.7 %all-gather.8.cloned.1.call-done = bf16[1024,512]{1,0:T(8,128)(2,1)} async-done(((bf16[32,512]{1,0:T(8,128)(2,1)}), bf16[1024,512]{1,0:T(8,128)(2,1)}) %all-gather.8.cloned.1.call-update) | async-done | bytes 1048592 | tf_op jit(solution)/shard_map/all_gather | solution.py:128
  130.4 55.0 %all-gather.12.cloned.1.call-done = bf16[1024,1024]{1,0:T(8,128)(2,1)} async-done(((bf16[32,1024]{1,0:T(8,128)(2,1)}), bf16[1024,1024]{1,0:T(8,128)(2,1)}) %all-gather.12.cloned.1.call-update) | async-done | bytes 2097168 | tf_op jit(solution)/shard_map/all_gather | solution.py:127
  195.3 15.4 all-to-all-done.1
  230.7 14.6 scatter_custom_fusion.1
  245.4 8.1 scatter_custom_fusion
  258.1 14.0 gather_fusion
  272.2 6.8 select_multiply_fusion
  279.0 4.8 all-to-all-start.3
  284.5 47.6 %all-gather.16.cloned.1.call-done = bf16[4,1024,512]{2,1,0:T(8,128)(2,1)} async-done(((bf16[4,256,512]{2,1,0:T(8,128)(2,1)}), bf16[4,1024,512]{2,1,0:T(8,128)(2,1)}) %all-gather.16.cloned.1.call-update) | async-done | bytes 4194320 | tf_op jit(solution)/shard_map/all_gather | solution.py:236
  332.1 23.2 %all-to-all-done.3 = bf16[8,384,1024]{2,1,0:T(8,128)(2,1)} async-done(((bf16[8,384,1024]{2,1,0:T(8,128)(2,1)}), bf16[8,384,1024]{2,1,0:T(8,128)(2,1)}, u32[]{:S(2)}, u32[]{:S(2)}) %all-to-all-start.3) | async-done | bytes 6291488 | tf_op jit(solution)/shard_map/all_to_all | solution.py:243
  355.4 10.2 fusion.30
  365.6 47.2 %all-gather.18.cloned.1.call-done = bf16[4,1024,512]{2,1,0:T(8,128)(2,1)} async-done(((bf16[4,256,512]{2,1,0:T(8,128)(2,1)}), bf16[4,1024,512]{2,1,0:T(8,128)(2,1)}) %all-gather.18.cloned.1.call-update) | async-done | bytes 4194320 | tf_op jit(solution)/shard_map/all_gather | solution.py:237
  412.8 13.4 fusion.19
  426.3 67.2 %all-gather.20.cloned.1.call-done = bf16[4,512,1024]{2,1,0:T(8,128)(2,1)} async-done(((bf16[4,512,256]{2,1,0:T(8,128)(2,1)}), bf16[4,512,1024]{2,1,0:T(8,128)(2,1)}) %all-gather.20.cloned.1.call-update) | async-done | bytes 4194320 | tf_op jit(solution)/shard_map/all_gather | solution.py:238
  493.4 6.6 convert_bitcast_fusion.1
  503.4 4.9 all-to-all-start.4
  508.5 14.3 gather_fusion.1
  522.8 70.1 %all_gather.36 = bf16[1024,32]{1,0:T(8,128)(2,1)S(1)} all-gather(bf16[32,32]{1,0:T(8,128)(2,1)S(1)} %copy-done.52), channel_id=1, replica_groups=mesh['fsdp'=8,'seq'=4] {'fsdp','seq'}, dimensions={0}, use_global_device_ids=true | all-gather | bytes 67584 | tf_op jit(solution)/shard_map/all_gather | solution.py:132
  593.2 14.6 gather_fusion.2
  611.4 8.1 scatter_custom_fusion.2
  619.5 5.5 multiply_convert_fusion
  625.0 74.3 %all_to_all.116 = bf16[8,384,1024]{2,1,0:T(8,128)(2,1)S(1)} all-to-all(bf16[8,384,1024]{2,1,0:T(8,128)(2,1)S(1)} %multiply_convert_fusion), channel_id=1, replica_groups=mesh['fsdp'=8,'seq'=4] {'fsdp'}, dimensions={0} | all-to-all | bytes 12582912 | tf_op jit(solution)/shard_map/all_to_all | solution.py:257
  701.9 5.0 bitcast_convert_fusion
  707.5 12.4 fusion.16
  721.6 8.8 bitcast_convert_fusion.2
  730.4 11.1 fusion.34
  741.6 12.9 fusion.13
  754.5 6.7 copy.219
  761.1 4.8 all-to-all-start.6
  766.2 9.2 bitcast_convert_fusion.1
  775.4 62.1 %all-to-all-done.6 = bf16[8,384,1024]{2,1,0:T(8,128)(2,1)} async-done(((bf16[8,384,1024]{2,1,0:T(8,128)(2,1)}), bf16[8,384,1024]{2,1,0:T(8,128)(2,1)}, u32[]{:S(2)}, u32[]{:S(2)}) %all-to-all-start.6) | async-done | bytes 6291488 | tf_op jit(solution)/shard_map/all_to_all | solution.py:267
  837.5 14.7 gather_fusion.3
  852.2 8.1 convert_reduce_fusion
  868.4 25.5 %all-to-all-done.7 = bf16[256,4,256]{0,2,1:T(8,128)(2,1)S(1)} async-done(((bf16[256,4,256]{0,2,1:T(8,128)(2,1)}), bf16[256,4,256]{0,2,1:T(8,128)(2,1)S(1)}, u32[]{:S(2)}, u32[]{:S(2)}) %all-to-all-start.7) | async-done | bytes 524320 | tf_op jit(solution)/shard_map/all_to_all | solution.py:306
  896.6 5.7 fusion.67
  902.3 6.4 fusion.78
  912.8 6.6 fusion.8
  920.8 5.4 fusion.5
  944.8 13.5 all-to-all-done.9
  976.4 15.4 all_to_all.117
  1002.0 42.4 %all-reduce.4 = (f32[1024]{0:T(1024)S(1)}, f32[1024]{0:T(1024)S(1)}) all-reduce(f32[1024]{0:T(1024)S(1)} %get-tuple-element.15, f32[1024]{0:T(1024)S(1)} %get-tuple-element.13), channel_id=2, replica_groups=mesh['fsdp'=8,'seq'=4] {'fsdp','seq'}, use_global_device_ids=true, to_apply=%region_25.27.clone | all-reduce | flops 2048 | bytes 16384
  1055.2 40.1 %reduce-scatter.17.cloned.1.call-done = f32[32,32]{1,0:T(8,128)} async-done(((f32[1024,32]{1,0:T(8,128)}), f32[32,32]{1,0:T(8,128)}) %reduce-scatter.17.cloned.1.call-update) | async-done | bytes 4112 | tf_op jit(solution)/shard_map/reduce_scatter | solution.py:382
  1095.3 139.0 %reduce-scatter.13.cloned.1.call-done = f32[32,512]{1,0:T(8,128)} async-done(((f32[1024,512]{1,0:T(8,128)}), f32[32,512]{1,0:T(8,128)}) %reduce-scatter.13.cloned.1.call-update) | async-done | bytes 65552 | tf_op jit(solution)/shard_map/reduce_scatter | solution.py:379
  1234.3 140.4 %reduce-scatter.11.cloned.1.call-done = f32[32,512]{1,0:T(8,128)} async-done(((f32[1024,512]{1,0:T(8,128)}), f32[32,512]{1,0:T(8,128)}) %reduce-scatter.11.cloned.1.call-update) | async-done | bytes 65552 | tf_op jit(solution)/shard_map/reduce_scatter | solution.py:378
  1374.7 150.0 %reduce-scatter.15.cloned.1.call-done = f32[32,1024]{1,0:T(8,128)} async-done(((f32[1024,1024]{1,0:T(8,128)}), f32[32,1024]{1,0:T(8,128)}) %reduce-scatter.15.cloned.1.call-update) | async-done | bytes 131088 | tf_op jit(solution)/shard_map/reduce_scatter | solution.py:380
  1524.7 149.9 %reduce-scatter.9.cloned.1.call-done = f32[32,1024]{1,0:T(8,128)} async-done(((f32[1024,1024]{1,0:T(8,128)}), f32[32,1024]{1,0:T(8,128)}) %reduce-scatter.9.cloned.1.call-update) | async-done | bytes 131088 | tf_op jit(solution)/shard_map/reduce_scatter | solution.py:377
  (301 shorter events, 140.0 us)
Async XLA Ops:
  7.2 117.8 %copy-start = (bf16[1,256,1024]{2,1,0:T(8,128)(2,1)S(1)}, bf16[1,256,1024]{2,1,0:T(8,128)(2,1)}, u32[]{:S(2)}) copy-start(bf16[1,256,1024]{2,1,0:T(8,128)(2,1)} %param.16) | copy-start | bytes 1572868
  7.2 61.7 %all-gather.10.cloned.1.call-start = ((), (), s32[]{:S(2)}) async-start(), calls=%async_computation.19 | async-start | bytes 1081344 | tf_op jit(solution)/shard_map/all_gather | solution.py:129
  7.9 115.6 %all-gather.8.cloned.1.call-start = ((), (), s32[]{:S(2)}) async-start(), calls=%async_computation.18 | async-start | bytes 1081344 | tf_op jit(solution)/shard_map/all_gather | solution.py:128
  8.7 176.8 %all-gather.12.cloned.1.call-start = ((), (), s32[]{:S(2)}) async-start(), calls=%async_computation.20 | async-start | bytes 2162688 | tf_op jit(solution)/shard_map/all_gather | solution.py:127
  9.4 245.0 %all-gather.14.cloned.1.call-start = ((), (), s32[]{:S(2)}) async-start(), calls=%async_computation.21 | async-start | bytes 2162688 | tf_op jit(solution)/shard_map/all_gather | solution.py:130
  10.0 322.2 %all-gather.16.cloned.1.call-start = ((), (), s32[]{:S(2)}) async-start(), calls=%async_computation.22 | async-start | bytes 5242880 | tf_op jit(solution)/shard_map/all_gather | solution.py:236
  10.6 402.3 %all-gather.18.cloned.1.call-start = ((), (), s32[]{:S(2)}) async-start(), calls=%async_computation.23 | async-start | bytes 5242880 | tf_op jit(solution)/shard_map/all_gather | solution.py:237
  11.2 114.7 %copy-start.55 = (f32[32]{0:T(128)}, f32[32]{0:T(128)S(1)}, u32[]{:S(2)}) copy-start(f32[32]{0:T(128)S(1)} %negate_power_fusion) | copy-start | bytes 388
  14.8 173.6 %copy-start.39 = (f32[256]{0:T(256)}, f32[256]{0:T(256)S(1)}, u32[]{:S(2)}) copy-start(f32[256]{0:T(256)S(1)} %get-tuple-element.54) | copy-start | bytes 3076
  58.5 129.9 %copy-start.34 = (f32[1024]{0:T(1024)}, f32[1024]{0:T(1024)S(1)}, u32[]{:S(2)}) copy-start(f32[1024]{0:T(1024)S(1)} %convert_element_type.222) | copy-start | bytes 12292
  58.5 199.1 %copy-start.37 = (f32[1024]{0:T(1024)}, f32[1024]{0:T(1024)S(1)}, u32[]{:S(2)}) copy-start(f32[1024]{0:T(1024)S(1)} %convert_element_type.236) | copy-start | bytes 12292
  126.7 67.4 %copy-start.49 = (s32[1,1024]{1,0:T(1,128)S(1)}, s32[1,1024]{1,0:T(1,128)}, u32[]{:S(2)}) copy-start(s32[1,1024]{1,0:T(1,128)} %param.18) | copy-start | bytes 12292
  126.7 63.4 %all-to-all-start = ((bf16[256,4,256]{2,0,1:T(8,128)(2,1)}), bf16[256,4,256]{2,0,1:T(8,128)(2,1)S(1)}, u32[]{:S(2)}, u32[]{:S(2)}) async-start(bf16[256,4,256]{2,0,1:T(8,128)(2,1)} %pad_maximum_fusion.2), calls=%async_computation | async-start | bytes 1048576 | tf_op jit(solution)/shard_map/all_to_all | solution.py:165
  190.2 20.5 %all-to-all-start.1 = ((bf16[256,4,256]{0,2,1:T(8,128)(2,1)}), bf16[256,4,256]{0,2,1:T(8,128)(2,1)S(1)}, u32[]{:S(2)}, u32[]{:S(2)}) async-start(bf16[256,4,256]{0,2,1:T(8,128)(2,1)} %bitcast.21), calls=%async_computation.1 | async-start | bytes 1048576 | tf_op jit(solution)/shard_map/all_to_all | solution.py:164
  194.9 23.7 %copy-start.18 = (pred[512,1024]{0,1:T(8,128)(4,1)}, pred[512,1024]{0,1:T(8,128)(4,1)S(1)}, u32[]{:S(2)}) copy-start(pred[512,1024]{0,1:T(8,128)(4,1)S(1)} %get-tuple-element.48) | copy-start | bytes 1572868
  194.9 26.2 %copy-start.20 = (pred[512,1024]{0,1:T(8,128)(4,1)}, pred[512,1024]{0,1:T(8,128)(4,1)S(1)}, u32[]{:S(2)}) copy-start(pred[512,1024]{0,1:T(8,128)(4,1)S(1)} %get-tuple-element.47) | copy-start | bytes 1572868
  195.1 18.1 %copy-start.15 = (bf16[1024,1,128]{0,2,1:T(8,128)(2,1)}, bf16[1024,1,128]{0,2,1:T(8,128)(2,1)S(1)}, u32[]{:S(2)}) copy-start(bf16[1024,1,128]{0,2,1:T(8,128)(2,1)S(1)} %copy.200) | copy-start | bytes 786436
  195.3 25.8 %copy-start.32 = (bf16[1024,1,128]{0,2,1:T(8,128)(2,1)}, bf16[1024,1,128]{0,2,1:T(8,128)(2,1)S(1)}, u32[]{:S(2)}) copy-start(bf16[1024,1,128]{0,2,1:T(8,128)(2,1)S(1)} %copy.199) | copy-start | bytes 786436
  227.0 26.4 %all-to-all-start.2 = ((bf16[4,2,32768]{2,1,0:T(2,128)(2,1)}), bf16[4,2,32768]{2,1,0:T(2,128)(2,1)S(1)}, u32[]{:S(2)}, u32[]{:S(2)}) async-start(bf16[4,2,32768]{2,1,0:T(2,128)(2,1)} %reshape.740), calls=%async_computation.2 | async-start | bytes 1048576 | tf_op jit(solution)/shard_map/all_to_all | solution.py:203
  254.3 17.8 %copy-start.10 = (bf16[256,4,1,256]{0,3,1,2:T(8,128)(2,1)}, bf16[256,4,1,256]{0,3,1,2:T(8,128)(2,1)S(1)}, u32[]{:S(2)}) copy-start(bf16[256,4,1,256]{0,3,1,2:T(8,128)(2,1)S(1)} %copy.207) | copy-start | bytes 1572868
  257.6 14.6 copy-start.50
  279.0 76.4 %all-to-all-start.3 = ((bf16[8,384,1024]{2,1,0:T(8,128)(2,1)}), bf16[8,384,1024]{2,1,0:T(8,128)(2,1)}, u32[]{:S(2)}, u32[]{:S(2)}) async-start(bf16[8,384,1024]{2,1,0:T(8,128)(2,1)} %select_multiply_fusion), calls=%async_computation.3 | async-start | bytes 12582912 | tf_op jit(solution)/shard_map/all_to_all | solution.py:243
  283.8 209.7 %all-gather.20.cloned.1.call-start = ((), (), s32[]{:S(2)}) async-start(), calls=%async_computation.24 | async-start | bytes 5242880 | tf_op jit(solution)/shard_map/all_gather | solution.py:238
  503.4 89.9 %all-to-all-start.4 = ((bf16[8,384,1024]{2,1,0:T(8,128)(2,1)}), bf16[8,384,1024]{2,1,0:T(8,128)(2,1)}, u32[]{:S(2)}, u32[]{:S(2)}) async-start(bf16[8,384,1024]{2,1,0:T(8,128)(2,1)} %bitcast.388), calls=%async_computation.4 | async-start | bytes 12582912 | tf_op jit(solution)/shard_map/all_to_all | solution.py:249
  508.2 538.6 %reduce-scatter.23.cloned.1.call-start = ((), (), s32[]{:S(2)}) async-start(), calls=%async_computation.32 | async-start | bytes 5242880 | tf_op jit(solution)/shard_map/reduce_scatter | solution.py:285
  508.5 14.3 copy-start.52
  508.5 84.7 %copy-start.36 = (s32[1,256,8]{1,2,0:T(8,128)S(1)}, s32[1,256,8]{1,2,0:T(8,128)}, u32[]{:S(2)}) copy-start(s32[1,256,8]{1,2,0:T(8,128)} %param.19) | copy-start | bytes 24580
  625.0 76.9 %copy-start.57 = (bf16[8,4,96,512]{3,2,0,1:T(8,128)(2,1)S(1)}, bf16[8,4,96,512]{3,2,0,1:T(8,128)(2,1)}, u32[]{:S(2)}) copy-start(bf16[8,4,96,512]{3,2,0,1:T(8,128)(2,1)} %get-tuple-element.63) | copy-start | bytes 9437188
  707.0 342.5 %reduce-scatter.19.cloned.1.call-start = ((), (), s32[]{:S(2)}) async-start(), calls=%async_computation.30 | async-start | bytes 5242880 | tf_op jit(solution)/shard_map/reduce_scatter | solution.py:279
  761.1 76.4 %all-to-all-start.6 = ((bf16[8,384,1024]{2,1,0:T(8,128)(2,1)}), bf16[8,384,1024]{2,1,0:T(8,128)(2,1)}, u32[]{:S(2)}, u32[]{:S(2)}) async-start(bf16[8,384,1024]{2,1,0:T(8,128)(2,1)} %bitcast.387), calls=%async_computation.6 | async-start | bytes 12582912 | tf_op jit(solution)/shard_map/all_to_all | solution.py:267
  765.9 286.5 %reduce-scatter.21.cloned.1.call-start = ((), (), s32[]{:S(2)}) async-start(), calls=%async_computation.31 | async-start | bytes 5242880 | tf_op jit(solution)/shard_map/reduce_scatter | solution.py:282
  852.2 8.1 copy-start.38
  852.2 8.1 copy-start.51
  852.2 8.8 copy-start.54
  862.2 34.4 %copy-start.21 = (pred[512,1024]{0,1:T(8,128)(4,1)S(1)}, pred[512,1024]{0,1:T(8,128)(4,1)}, u32[]{:S(2)}) copy-start(pred[512,1024]{0,1:T(8,128)(4,1)} %copy-done.20) | copy-start | bytes 1572868
  864.0 29.9 %all-to-all-start.7 = ((bf16[256,4,256]{0,2,1:T(8,128)(2,1)}), bf16[256,4,256]{0,2,1:T(8,128)(2,1)S(1)}, u32[]{:S(2)}, u32[]{:S(2)}) async-start(bf16[256,4,256]{0,2,1:T(8,128)(2,1)} %bitcast.70), calls=%async_computation.7 | async-start | bytes 1048576 | tf_op jit(solution)/shard_map/all_to_all | solution.py:306
  868.3 59.3 %copy-start.22 = (f32[1024,32]{0,1:T(8,128)}, f32[1024,32]{0,1:T(8,128)S(1)}, u32[]{:S(2)}) copy-start(f32[1024,32]{0,1:T(8,128)S(1)} %get-tuple-element.46) | copy-start | bytes 393220
  895.1 15.6 copy-start.27
  928.3 32.6 %copy-start.1 = (bf16[1,256,1024]{2,1,0:T(8,128)(2,1)S(1)}, bf16[1,256,1024]{2,1,0:T(8,128)(2,1)}, u32[]{:S(2)}) copy-start(bf16[1,256,1024]{2,1,0:T(8,128)(2,1)} %param.16) | copy-start | bytes 1572868
  928.3 32.7 %copy-start.35 = (f32[1024]{0:T(1024)S(1)}, f32[1024]{0:T(1024)}, u32[]{:S(2)}) copy-start(f32[1024]{0:T(1024)} %copy-done.34) | copy-start | bytes 12292
  928.3 32.7 %copy-start.40 = (f32[256]{0:T(256)S(1)}, f32[256]{0:T(256)}, u32[]{:S(2)}) copy-start(f32[256]{0:T(256)} %copy-done.39) | copy-start | bytes 3076
  939.4 18.9 %all-to-all-start.9 = ((bf16[4,2,32768]{2,1,0:T(2,128)(2,1)}), bf16[4,2,32768]{2,1,0:T(2,128)(2,1)}, u32[]{:S(2)}, u32[]{:S(2)}) async-start(bf16[4,2,32768]{2,1,0:T(2,128)(2,1)} %reshape.744), calls=%async_computation.9 | async-start | bytes 1048576 | tf_op jit(solution)/shard_map/all_to_all | solution.py:358
  943.6 151.7 %reduce-scatter.17.cloned.1.call-start = ((), (), s32[]{:S(2)}) async-start(), calls=%async_computation.29 | async-start | bytes 540672 | tf_op jit(solution)/shard_map/reduce_scatter | solution.py:382
  944.8 289.5 %reduce-scatter.13.cloned.1.call-start = ((), (), s32[]{:S(2)}) async-start(), calls=%async_computation.27 | async-start | bytes 2162688 | tf_op jit(solution)/shard_map/reduce_scatter | solution.py:379
  962.9 411.7 %reduce-scatter.11.cloned.1.call-start = ((), (), s32[]{:S(2)}) async-start(), calls=%async_computation.26 | async-start | bytes 2162688 | tf_op jit(solution)/shard_map/reduce_scatter | solution.py:378
  965.8 558.9 %reduce-scatter.15.cloned.1.call-start = ((), (), s32[]{:S(2)}) async-start(), calls=%async_computation.28 | async-start | bytes 4325376 | tf_op jit(solution)/shard_map/reduce_scatter | solution.py:380
  968.6 706.0 %reduce-scatter.9.cloned.1.call-start = ((), (), s32[]{:S(2)}) async-start(), calls=%async_computation.25 | async-start | bytes 4325376 | tf_op jit(solution)/shard_map/reduce_scatter | solution.py:377
  997.3 48.2 %copy-start.53 = (f32[256]{0:T(256)S(1)}, f32[256]{0:T(256)}, u32[]{:S(2)}) copy-start(f32[256]{0:T(256)} %get-tuple-element.53) | copy-start | bytes 3076
  (33 other events, 154.6 us)
Sparse Core Ops, SparseCore 0:
  11.0 56.6 all-gather.9
  70.6 52.8 all-gather.7
  126.5 58.9 all-gather.11
  188.3 61.9 all-gather.13
  251.7 80.4 all-gather.15
  333.6 79.2 all-gather.17
  414.4 79.0 all-gather.19
  707.1 73.0 reduce-scatter.22
  782.6 77.2 reduce-scatter.18
  862.0 85.9 reduce-scatter.20
  950.8 144.4 reduce-scatter.16
  1098.0 136.2 reduce-scatter.12
  1237.1 137.4 reduce-scatter.10
  1377.4 147.2 reduce-scatter.14
  1527.4 147.2 reduce-scatter.8
where the time goes:
time: 1690 us; the launch traced here: 1680 us
  waiting for transfers between devices  1030 us (61%)
  blocking collectives  244 us (14%)
  matrix products  153 us (9%)
  local copies, waits for them, and re-layouts  133 us (8%)
  other arithmetic  66.9 us (4%)
  starting transfers between devices  35.1 us (2%)
    reduce_scatter x1, waiting for transfers between devices, on_device(): lax.psum_scatter(grad_out, ('fsdp', 'seq'), scatter_dimension=0, tiled=True)  150 us
    reduce_scatter x1, waiting for transfers between devices, on_device(): lax.psum_scatter(grad_query, ('fsdp', 'seq'), scatter_dimension=0, tiled=...  150 us
    reduce_scatter x1, waiting for transfers between devices, on_device(): lax.psum_scatter(grad_key, ('fsdp', 'seq'), scatter_dimension=0, tiled=True)  140 us
    reduce_scatter x1, waiting for transfers between devices, on_device(): lax.psum_scatter(grad_value, ('fsdp', 'seq'), scatter_dimension=0, tiled=...  139 us
    unnamed x2, blocking collectives  84.4 us
    all_to_all x1, blocking collectives, on_device(): lax.all_to_all(d_slot.reshape(n_fsdp, local_exp * slot_cap, width), 'fsdp...  74.3 us
    all_gather x1, blocking collectives, on_device(): lax.all_gather(w_router, ('fsdp', 'seq'), axis=0, tiled=True)  70.1 us
    all_gather x1, waiting for transfers between devices, on_device(): lax.all_gather(w_down, 'seq', axis=2, tiled=True)  67.2 us
  transfers between devices with their start and end apart: 23, of which 15 were waited for; matrix products, arithmetic and copies ran while one was open for 18% of the time, Pallas kernels for 0%

commit v1 on v0

v1 whole, which is shorter than its diff:
```python
import jax
import jax.numpy as jnp
from jax import lax
from jax.sharding import PartitionSpec as P

HD = 64


EPS = 1e-06
ATTN_MULT = 0.015625
RESID_MULT = 0.22
THETA = 10000.0
NEG_FILL = -1e30


def rope_tables(positions, head_dim):
    half_dim = head_dim // 2
    frequency = THETA ** (-(jnp.arange(half_dim, dtype=jnp.float32) * 2.0 / head_dim))
    phases = positions.astype(jnp.float32)[:, None] * frequency[None, :]
    return (jnp.cos(phases), jnp.sin(phases))


def rotate(values, cosine, sine_tab):
    half_dim = values.shape[-1] // 2
    first_half = values[..., :half_dim]
    second_half = values[..., half_dim:]
    cos_b = cosine[:, None, :]
    sin_b = sine_tab[:, None, :]
    return jnp.concatenate(
        [first_half * cos_b - second_half * sin_b, second_half * cos_b + first_half * sin_b],
        axis=-1,
    )


def unrotate(grad_vals, cosine, sine_tab):
    half_dim = grad_vals.shape[-1] // 2
    first_half = grad_vals[..., :half_dim]
    second_half = grad_vals[..., half_dim:]
    cos_b = cosine[:, None, :]
    sin_b = sine_tab[:, None, :]
    return jnp.concatenate(
        [first_half * cos_b + second_half * sin_b, second_half * cos_b - first_half * sin_b],
        axis=-1,
    )


def rms_scale(values):
    return lax.rsqrt(jnp.mean(values * values, axis=-1, keepdims=True) + EPS)


def norm_backward(inputs, scale, gain, d_normed):
    upstream = gain * d_normed
    d_inputs = scale * upstream - inputs * scale**3 * jnp.mean(
        upstream * inputs, axis=-1, keepdims=True
    )
    d_gain = jnp.sum(d_normed * inputs * scale, axis=0)
    return (d_inputs, d_gain)


def on_device(
    hidden_in,
    cotangent,
    doc_ids,
    routes,
    gain_attn,
    w_query,
    w_key,
    w_value,
    w_out,
    gain_ffn,
    w_router,
    w_gate,
    w_up,
    w_down,
):
    n_seq = lax.axis_size("seq")
    n_fsdp = lax.axis_size("fsdp")
    tok_rows = hidden_in.shape[1]
    width = hidden_in.shape[2]
    seq_len = tok_rows * n_seq
    top_k = routes.shape[2]
    n_expert = w_router.shape[1]
    local_exp = w_gate.shape[0]
    head_dim = HD
    q_width = w_query.shape[1]
    kv_width = w_key.shape[1]
    heads_here = q_width // head_dim // n_seq
    kv_here = kv_width // head_dim // n_seq
    group_size = heads_here // kv_here
    slot_cap = 3 * tok_rows * top_k // (2 * n_expert)
    f32, bf16 = jnp.float32, jnp.bfloat16
    row_own = w_query.shape[0]
    model = row_own * n_fsdp * n_seq

    def column(gain):
        return jnp.pad(gain[:, None], ((0, 0), (0, 127)))

    packed = jnp.concatenate(
        [
            w_query,
            w_key,
            w_value,
            column(gain_attn),
            w_out,
            jnp.pad(w_router, ((0, 0), (0, 128 - n_expert % 128))),
            column(gain_ffn),
        ],
        axis=1,
    )
    full = lax.all_gather(packed, ("fsdp", "seq"), axis=0, tiled=True)
    qkv_width = q_width + 2 * kv_width
    out_at = qkv_width + 128
    router_at = out_at + w_out.shape[1]
    gain_at = packed.shape[1] - 128
    full_qkv = full[:, :qkv_width]
    gain_one = full[:, qkv_width].astype(f32)
    full_out = full[:, out_at:router_at]
    full_router = full[:, router_at : router_at + n_expert]
    gain_two = full[:, gain_at].astype(f32)
    gathered_gate, gathered_up, gathered_down = (
        lax.all_gather(w_gate, "seq", axis=1, tiled=True),
        lax.all_gather(w_up, "seq", axis=1, tiled=True),
        lax.all_gather(w_down, "seq", axis=2, tiled=True),
    )

    def to_all(block):
        return lax.all_to_all(
            jnp.broadcast_to(block[None], (n_fsdp,) + block.shape),
            "fsdp",
            split_axis=0,
            concat_axis=0,
            tiled=True,
        )

    grad_in = cotangent[0]
    d_moe_all = to_all((RESID_MULT * grad_in).astype(bf16))
    routes_all = to_all(routes[0].T)
    tokens = hidden_in[0].astype(f32)
    scale_one = rms_scale(tokens)
    normed_one = (tokens * scale_one * gain_one).astype(bf16)
    tok_pos = lax.axis_index("seq") * tok_rows + jnp.arange(tok_rows, dtype=jnp.int32)
    cos_tok, sin_tok = rope_tables(tok_pos, head_dim)
    qkv = jnp.dot(normed_one, full_qkv, preferred_element_type=f32)
    query = qkv[:, :q_width].reshape(tok_rows, -1, head_dim)
    keys_tok = qkv[:, q_width : q_width + kv_width].reshape(tok_rows, -1, head_dim)
    query = (
        rotate(query, cos_tok, sin_tok).astype(bf16).reshape(tok_rows, n_seq, heads_here * head_dim)
    )
    keys_tok = (
        rotate(keys_tok, cos_tok, sin_tok).astype(bf16).reshape(tok_rows, n_seq, kv_here * head_dim)
    )
    values_tok = qkv[:, q_width + kv_width :].astype(bf16)
    key_value = jnp.concatenate(
        [query, keys_tok, values_tok.reshape(tok_rows, n_seq, kv_here * head_dim)], axis=-1
    )
    recv = lax.all_to_all(key_value, "seq", split_axis=1, concat_axis=0, tiled=True)[:, 0]
    q_here = heads_here * head_dim
    k_end = q_here + kv_here * head_dim
    q_heads = recv[:, :q_here].reshape(seq_len, kv_here, group_size, head_dim)
    k_heads = recv[:, q_here:k_end].reshape(seq_len, kv_here, head_dim)
    v_heads = recv[:, k_end:].reshape(seq_len, kv_here, head_dim)
    doc_row = doc_ids[0]
    key_pos = jnp.arange(seq_len, dtype=jnp.int32)
    block_rows = min(512, seq_len)
    starts = list(range(0, seq_len, block_rows))

    def block_scores(row_start):
        row_end = row_start + block_rows
        q_blk = q_heads[row_start:row_end]
        query_pos = row_start + jnp.arange(block_rows, dtype=jnp.int32)
        allowed = (query_pos[:, None] >= key_pos[None, :row_end]) & (
            doc_row[row_start:row_end][:, None] == doc_row[None, :row_end]
        )
        scores = (
            jnp.einsum("qkgd,skd->kgqs", q_blk, k_heads[:row_end], preferred_element_type=f32)
            * ATTN_MULT
        )
        return (q_blk, jnp.where(allowed[None, None], scores, NEG_FILL))

    attn_parts = []
    lse_parts = []
    for row_start in starts:
        q_blk, scores = block_scores(row_start)
        top_val = jnp.max(scores, axis=-1, keepdims=True)
        expo_vals = jnp.exp(scores - top_val)
        row_total = jnp.sum(expo_vals, axis=-1, keepdims=True)
        lse_parts.append(top_val[..., 0] + jnp.log(row_total[..., 0]))
        prob_vals = (expo_vals / row_total).astype(bf16)
        attn_parts.append(
            jnp.einsum(
                "kgqs,skd->qkgd",
                prob_vals,
                v_heads[: row_start + block_rows],
                preferred_element_type=f32,
            ).astype(bf16)
        )
    attn_heads = jnp.concatenate(attn_parts, axis=0)
    attn_tok = lax.all_to_all(
        attn_heads.reshape(seq_len, 1, q_here),
        "seq",
        split_axis=0,
        concat_axis=1,
        tiled=True,
    ).reshape(tok_rows, q_width)
    branch = jnp.dot(attn_tok, full_out, preferred_element_type=f32)
    resid = tokens + RESID_MULT * branch
    scale_two = rms_scale(resid)
    normed_two = (resid * scale_two * gain_two).astype(bf16)
    tok_all = to_all(normed_two)

    def dense_gates(logits, route_kt):
        experts = jnp.arange(n_expert, dtype=jnp.int32)
        picked = jnp.any(route_kt[..., None] == experts, axis=-3)
        top_val = jnp.max(jnp.where(picked, logits, NEG_FILL), axis=-1, keepdims=True)
        expo_vals = jnp.where(picked, jnp.exp(jnp.where(picked, logits - top_val, 0.0)), 0.0)
        return picked, expo_vals / jnp.sum(expo_vals, axis=-1, keepdims=True)

    logits_own = jnp.dot(normed_two, full_router, preferred_element_type=f32)
    _, gates = dense_gates(logits_own, routes[0].T)
    first = lax.axis_index("fsdp") * local_exp
    picked_all, gates_all = dense_gates(
        jnp.einsum("std,de->ste", tok_all, full_router, preferred_element_type=f32), routes_all
    )
    own_picked = jnp.transpose(
        lax.dynamic_slice_in_dim(picked_all, first, local_exp, axis=2), (0, 2, 1)
    )
    own_gates = jnp.transpose(
        lax.dynamic_slice_in_dim(gates_all, first, local_exp, axis=2), (0, 2, 1)
    )
    earlier = (
        jnp.arange(tok_rows, dtype=jnp.int32)[:, None]
        < jnp.arange(tok_rows, dtype=jnp.int32)[None, :]
    ).astype(bf16)
    place = jnp.einsum(
        "seu,ut->set", own_picked.astype(bf16), earlier, preferred_element_type=f32
    ).astype(jnp.int32)
    place = jnp.where(own_picked, place, -1)
    slot_hit = place[:, :, None, :] == jnp.arange(slot_cap, dtype=jnp.int32)[:, None]
    slot_map = slot_hit.astype(bf16)
    slot_gate = jnp.sum(jnp.where(slot_hit, own_gates[:, :, None, :], 0.0), axis=-1)
    slot_gate = jnp.transpose(slot_gate, (1, 0, 2)).reshape(local_exp, n_fsdp * slot_cap, 1)
    slot_flat = slot_map.reshape(n_fsdp, local_exp * slot_cap, tok_rows)

    def to_slots(rows):
        found = jnp.einsum("sjt,std->sjd", slot_flat, rows, preferred_element_type=f32)
        found = found.astype(bf16).reshape(n_fsdp, local_exp, slot_cap, width)
        return jnp.transpose(found, (1, 0, 2, 3)).reshape(local_exp, n_fsdp * slot_cap, width)

    def from_slots(rows):
        rows = rows.reshape(local_exp, n_fsdp, slot_cap, width)
        rows = jnp.transpose(rows, (1, 0, 2, 3)).reshape(n_fsdp, local_exp * slot_cap, width)
        part = jnp.einsum("sjt,sjd->std", slot_flat, rows, preferred_element_type=f32)
        part = lax.all_to_all(part.astype(bf16), "fsdp", split_axis=0, concat_axis=0, tiled=True)
        return jnp.sum(part.astype(f32), axis=0)

    d_rows = to_slots(d_moe_all)
    inbound = to_slots(tok_all)
    pre_gate = jnp.einsum("ead,edf->eaf", inbound, gathered_gate, preferred_element_type=f32)
    pre_up = jnp.einsum("ead,edf->eaf", inbound, gathered_up, preferred_element_type=f32)
    sigm = jax.nn.sigmoid(pre_gate)
    act = pre_gate * sigm * pre_up
    act_gated = (act * slot_gate).astype(bf16)
    d_plain = jnp.einsum("ead,efd->eaf", d_rows, gathered_down, preferred_element_type=f32)
    slot_d_gate = jnp.sum(act * d_plain, axis=-1)
    d_act = d_plain * slot_gate
    d_up = (d_act * pre_gate * sigm).astype(bf16)
    d_pre_gate = (d_act * pre_up * sigm * (1.0 + pre_gate * (1.0 - sigm))).astype(bf16)
    slot_d_gate = jnp.transpose(
        slot_d_gate.reshape(local_exp, n_fsdp, slot_cap), (1, 0, 2)
    )
    d_gates_part = jnp.sum(jnp.where(slot_hit, slot_d_gate[..., None], 0.0), axis=2)
    d_gates = lax.all_to_all(d_gates_part, "fsdp", split_axis=0, concat_axis=0, tiled=True)
    d_gates = d_gates.reshape(n_expert, tok_rows).T
    d_inputs = (
        jnp.einsum("eaf,edf->ead", d_pre_gate, gathered_gate, preferred_element_type=f32)
        + jnp.einsum("eaf,edf->ead", d_up, gathered_up, preferred_element_type=f32)
    ).astype(bf16)
    d_from_experts = from_slots(d_inputs)
    expert_out = jnp.einsum("eaf,efd->ead", act_gated, gathered_down, preferred_element_type=f32)
    output = resid + RESID_MULT * from_slots(expert_out.astype(bf16))
    grad_gate = jnp.einsum("ead,eaf->edf", inbound, d_pre_gate, preferred_element_type=f32)
    grad_up = jnp.einsum("ead,eaf->edf", inbound, d_up, preferred_element_type=f32)
    grad_down = jnp.einsum("ead,eaf->efd", d_rows, act_gated, preferred_element_type=f32)

    def sum_seq(grad, axis):
        shape = grad.shape[:axis] + (n_seq, grad.shape[axis] // n_seq) + grad.shape[axis + 1 :]
        parts = jnp.moveaxis(grad.astype(bf16).reshape(shape), axis, 0)
        parts = lax.all_to_all(parts, "seq", split_axis=0, concat_axis=0, tiled=True)
        return jnp.sum(parts.astype(f32), axis=0)

    owned_gate, owned_up, owned_down = (
        sum_seq(grad_gate, 1),
        sum_seq(grad_up, 1),
        sum_seq(grad_down, 2),
    )

    def sum_all(grad):
        parts = lax.all_to_all(
            grad.astype(bf16).reshape(n_fsdp, model // n_fsdp, -1),
            "fsdp",
            split_axis=0,
            concat_axis=0,
            tiled=True,
        )
        part = jnp.sum(parts.astype(f32), axis=0).astype(bf16)
        parts = lax.all_to_all(
            part.reshape(n_seq, row_own, -1), "seq", split_axis=0, concat_axis=0, tiled=True
        )
        return jnp.sum(parts.astype(f32), axis=0)

    d_chosen = gates * (d_gates - jnp.sum(gates * d_gates, axis=-1, keepdims=True))
    d_logits = d_chosen.astype(bf16)
    d_normed_two = d_from_experts + jnp.einsum(
        "te,de->td", d_logits, full_router, preferred_element_type=f32
    )
    grad_router = jnp.einsum("td,te->de", normed_two, d_logits, preferred_element_type=f32)
    d_norm_two, grad_gain_two = norm_backward(resid, scale_two, gain_two, d_normed_two)
    d_resid = grad_in + d_norm_two
    d_branch = (RESID_MULT * d_resid).astype(bf16)
    grad_out = jnp.einsum("tq,td->qd", attn_tok, d_branch, preferred_element_type=f32)
    d_attn = jnp.einsum("td,qd->tq", d_branch, full_out, preferred_element_type=f32).astype(bf16)
    own_early = sum_all(
        jnp.concatenate(
            [grad_out, jnp.pad(grad_router, ((0, 0), (0, 127 - n_expert))), grad_gain_two[:, None]],
            axis=1,
        )
    )
    d_heads = lax.all_to_all(
        d_attn.reshape(tok_rows, n_seq, q_here),
        "seq",
        split_axis=1,
        concat_axis=0,
        tiled=True,
    ).reshape(seq_len, kv_here, group_size, head_dim)
    d_query_parts = []
    d_key_sum = jnp.zeros((seq_len, kv_here, head_dim), f32)
    d_val_sum = jnp.zeros((seq_len, kv_here, head_dim), f32)
    for step, row_start in enumerate(starts):
        row_end = row_start + block_rows
        q_blk, scores = block_scores(row_start)
        prob_vals = jnp.exp(scores - lse_parts[step][..., None])
        d_out_blk = d_heads[row_start:row_end]
        attn_blk = attn_heads[row_start:row_end]
        d_val_sum = d_val_sum.at[:row_end].add(
            jnp.einsum(
                "kgqs,qkgd->skd", prob_vals.astype(bf16), d_out_blk, preferred_element_type=f32
            )
        )
        d_prob = jnp.einsum(
            "qkgd,skd->kgqs", d_out_blk, v_heads[:row_end], preferred_element_type=f32
        )
        row_delta = jnp.transpose(
            jnp.sum(d_out_blk.astype(f32) * attn_blk.astype(f32), axis=-1), (1, 2, 0)
        )
        d_score = (prob_vals * (d_prob - row_delta[..., None]) * ATTN_MULT).astype(bf16)
        d_query_parts.append(
            jnp.einsum("kgqs,skd->qkgd", d_score, k_heads[:row_end], preferred_element_type=f32)
        )
        d_key_sum = d_key_sum.at[:row_end].add(
            jnp.einsum("kgqs,qkgd->skd", d_score, q_blk, preferred_element_type=f32)
        )
    cos_full, sin_full = rope_tables(key_pos, head_dim)
    d_query_all = jnp.concatenate(d_query_parts, axis=0).reshape(seq_len, heads_here, head_dim)
    d_query_rot = unrotate(d_query_all, cos_full, sin_full).astype(bf16).reshape(seq_len, 1, q_here)
    d_key_rot = (
        unrotate(d_key_sum, cos_full, sin_full).astype(bf16).reshape(seq_len, 1, kv_here * head_dim)
    )
    d_val_low = d_val_sum.astype(bf16).reshape(seq_len, 1, kv_here * head_dim)
    d_recv = lax.all_to_all(
        jnp.concatenate([d_query_rot, d_key_rot, d_val_low], axis=-1),
        "seq",
        split_axis=0,
        concat_axis=1,
        tiled=True,
    )
    d_qkv = jnp.concatenate(
        [
            d_recv[:, :, :q_here].reshape(tok_rows, q_width),
            d_recv[:, :, q_here:k_end].reshape(tok_rows, kv_width),
            d_recv[:, :, k_end:].reshape(tok_rows, kv_width),
        ],
        axis=1,
    )
    d_normed_one = jnp.einsum("tq,dq->td", d_qkv, full_qkv, preferred_element_type=f32)
    grad_qkv = jnp.einsum("td,tq->dq", normed_one, d_qkv, preferred_element_type=f32)
    d_norm_one, grad_gain_one = norm_backward(tokens, scale_one, gain_one, d_normed_one)
    d_input = d_resid + d_norm_one
    own_late = sum_all(
        jnp.concatenate([grad_qkv, jnp.pad(grad_gain_one[:, None], ((0, 0), (0, 127)))], axis=1)
    )
    return (
        output[None],
        d_input[None],
        own_late[:, qkv_width],
        own_late[:, :q_width],
        own_late[:, q_width : q_width + kv_width],
        own_late[:, q_width + kv_width : qkv_width],
        own_early[:, :width],
        own_early[:, width + 127],
        own_early[:, width : width + n_expert],
        owned_gate,
        owned_up,
        owned_down,
    )


def solution(mesh):
    placed = (
        P("fsdp", "seq", None),
        P("fsdp", "seq", None),
        P("fsdp", None),
        P("fsdp", "seq", None),
        P(("fsdp", "seq")),
        P(("fsdp", "seq"), None),
        P(("fsdp", "seq"), None),
        P(("fsdp", "seq"), None),
        P(("fsdp", "seq"), None),
        P(("fsdp", "seq")),
        P(("fsdp", "seq"), None),
        P("fsdp", "seq", None),
        P("fsdp", "seq", None),
        P("fsdp", None, "seq"),
    )
    return jax.shard_map(
        on_device,
        mesh=mesh,
        in_specs=placed,
        out_specs=(
            P("fsdp", "seq", None),
            P("fsdp", "seq", None),
            P(("fsdp", "seq")),
            P(("fsdp", "seq"), None),
            P(("fsdp", "seq"), None),
            P(("fsdp", "seq"), None),
            P(("fsdp", "seq"), None),
            P(("fsdp", "seq")),
            P(("fsdp", "seq"), None),
            P("fsdp", "seq", None),
            P("fsdp", "seq", None),
            P("fsdp", None, "seq"),
        ),
        check_vma=False,
    )
```

time: 1690 us -> 1010 us (0.60)
  waiting for transfers between devices: 1030 us -> 632 us
  blocking collectives: 244 us -> 0 us
  local copies, waits for them, and re-layouts: 133 us -> 68.3 us
  starting transfers between devices: 35.1 us -> 74.5 us
    reduce_scatter x8 -> x0, waiting for transfers between devices: 619 us -> none  [the longest x1 150 us: on_device(): lax.psum_scatter(grad_out, ('fsdp', 'seq'), scatter_dimension=0, tiled=True)]
    all_to_all x7 -> x16, waiting for transfers between devices: 140 us -> 492 us  [the longest x3 249 us: sum_seq(): lax.all_to_all(parts, 'seq', split_axis=0, concat_axis=0, tiled=True)]
    all_to_all x2 -> x0, blocking collectives: 89.7 us -> none  [the longest x1 74.3 us: on_device(): lax.all_to_all(d_slot.reshape(n_fsdp, local_exp * slot_cap, width), 'fsdp...]
    unnamed x2 -> x0, blocking collectives: 84.4 us -> none
    all_gather x1 -> x0, blocking collectives: 70.1 us -> none  [on_device(): lax.all_gather(w_router, ('fsdp', 'seq'), axis=0, tiled=True)]
    gather x4 -> x0, local copies, waits for them, and re-layouts: 57.5 us -> none  [the longest x1 14.7 us: on_device(): jnp.take(d_back, slot_of, axis=0).reshape(tok_rows, top_k, width)]
    all_to_all x1, waiting for transfers between devices: 0.01 us -> 57 us  [on_device(): lax.all_to_all(key_value, 'seq', split_axis=1, concat_axis=0, tiled=True)]
    all_gather x1, waiting for transfers between devices: 67.2 us -> 10.4 us  [on_device(): lax.all_gather(w_down, 'seq', axis=2, tiled=True)]
  transfers between devices with their start and end apart: 23 -> 21, of which waited for: 15 -> 15; matrix products, arithmetic and copies ran while one was open for 18% -> 24% of each run, Pallas kernels for 0% -> 0%
where the time goes in v1:
time: 1010 us
  waiting for transfers between devices  632 us (63%)
  matrix products  156 us (15%)
  starting transfers between devices  74.5 us (7%)
  local copies, waits for them, and re-layouts  68.3 us (7%)
  other arithmetic  61 us (6%)
  between operations  15.6 us (2%)
    all_to_all x3, waiting for transfers between devices, sum_seq(): lax.all_to_all(parts, 'seq', split_axis=0, concat_axis=0, tiled=True)  249 us
    all_to_all x3, waiting for transfers between devices, to_all(): lax.all_to_all(jnp.broadcast_to(block[None], (n_fsdp,) + block.shape), 'f...  83.4 us
    all_gather x1, waiting for transfers between devices, on_device(): full = lax.all_gather(packed, ('fsdp', 'seq'), axis=0, tiled=True)  71.6 us
    all_to_all x2, waiting for transfers between devices, from_slots(): lax.all_to_all(part.astype(bf16), 'fsdp', split_axis=0, concat_axis=0, ti...  69.3 us
    all_to_all x1, waiting for transfers between devices, on_device(): lax.all_to_all(key_value, 'seq', split_axis=1, concat_axis=0, tiled=True)  57 us
    all_to_all x2, waiting for transfers between devices, sum_all(): lax.all_to_all(grad.astype(bf16).reshape(n_fsdp, model // n_fsdp, -1), 'f...  42.3 us
    all_to_all x1, waiting for transfers between devices, on_device(): lax.all_to_all(jnp.concatenate([d_query_rot, d_key_rot, d_val_low], axis=...  25.5 us
    unnamed x165, local copies, waits for them, and re-layouts  24.1 us
  transfers between devices with their start and end apart: 21, of which 15 were waited for; matrix products, arithmetic and copies ran while one was open for 24% of the time, Pallas kernels for 0%

profile of v1, /device:TPU:0, one launch (start us, length us, event | category | flops | bytes accessed | tf_op | source)
XLA Modules:
  0.0 1006.8 jit_solution(12209776214409809186)
XLA Ops:
  16.8 71.6 %all-gather.5.cloned.1.call-done = bf16[1024,3456]{1,0:T(8,128)(2,1)} async-done(((bf16[32,3456]{1,0:T(8,128)(2,1)}), bf16[1024,3456]{1,0:T(8,128)(2,1)}) %all-gather.5.cloned.1.call-update) | async-done | bytes 7077904 | tf_op jit(solution)/shard_map/all_gather | solution.py:110
  101.3 57.0 %all-to-all-done = bf16[256,4,512]{0,2,1:T(8,128)(2,1)S(1)} async-done(((bf16[256,4,512]{0,2,1:T(8,128)(2,1)}), bf16[256,4,512]{0,2,1:T(8,128)(2,1)S(1)}, u32[]{:S(2)}, u32[]{:S(2)}) %all-to-all-start) | async-done | bytes 1048608 | tf_op jit(solution)/shard_map/all_to_all | solution.py:156
  158.9 4.5 all-to-all-start.2
  175.3 4.9 fusion.59
  187.2 17.3 %all-to-all-done.1 = bf16[4,2,32768]{2,1,0:T(2,128)(2,1)S(1)} async-done(((bf16[4,2,32768]{2,1,0:T(2,128)(2,1)}), bf16[4,2,32768]{2,1,0:T(2,128)(2,1)S(1)}, u32[]{:S(2)}, u32[]{:S(2)}) %all-to-all-start.1) | async-done | bytes 524320 | tf_op jit(solution)/shard_map/all_to_all | solution.py:198
  207.0 4.6 all-to-all-start.5
  216.3 44.4 %all-to-all-done.5 = bf16[8,256,1024]{2,1,0:T(8,128)(2,1)} async-done(((bf16[8,256,1024]{2,1,0:T(8,128)(2,1)}), bf16[8,256,1024]{2,1,0:T(8,128)(2,1)}, u32[]{:S(2)}, u32[]{:S(2)}) %all-to-all-start.5) | async-done | bytes 4194336 | tf_op jit(solution)/shard_map/all_to_all | solution.py:127
  263.3 4.6 all-to-all-start.3
  270.4 4.3 convolution_convert_fusion.1
  278.0 38.9 %all-to-all-done.3 = bf16[8,256,1024]{2,1,0:T(8,128)(2,1)} async-done(((bf16[8,256,1024]{2,1,0:T(8,128)(2,1)}), bf16[8,256,1024]{2,1,0:T(8,128)(2,1)}, u32[]{:S(2)}, u32[]{:S(2)}) %all-to-all-start.3) | async-done | bytes 4194336 | tf_op jit(solution)/shard_map/all_to_all | solution.py:127
  316.9 4.0 convolution_convert_fusion.2
  328.8 10.1 %fusion.113 = f32[4,768,512]{1,2,0:T(8,128)} fusion(bf16[4,768,1024]{2,1,0:T(8,128)(2,1)} %bitcast.329, bf16[4,1024,512]{1,2,0:T(8,128)(2,1)} %all-gather.9.cloned.1.call-done), kind=kOutput, calls=%fused_computation.224 | convolution fusion | flops 3221225472 | bytes 16777216 | tf_op jit(solution)/shard_map/ead,edf->eaf/dot_general | solution.py:259
  339.0 10.2 %fusion.112 = f32[4,768,512]{1,2,0:T(8,128)} fusion(bf16[4,768,1024]{2,1,0:T(8,128)(2,1)} %bitcast.330, bf16[4,1024,512]{1,2,0:T(8,128)(2,1)} %all-gather.7.cloned.1.call-done), kind=kOutput, calls=%fused_computation.223 | convolution fusion | flops 3221225472 | bytes 16777216 | tf_op jit(solution)/shard_map/ead,edf->eaf/dot_general | solution.py:258
  349.2 10.4 %all-gather.11.cloned.1.call-done = bf16[4,512,1024]{2,1,0:T(8,128)(2,1)} async-done(((bf16[4,512,256]{2,1,0:T(8,128)(2,1)}), bf16[4,512,1024]{2,1,0:T(8,128)(2,1)}) %all-gather.11.cloned.1.call-update) | async-done | bytes 4194320 | tf_op jit(solution)/shard_map/all_gather | solution.py:123
  359.6 14.3 %multiply_reduce_fusion = (f32[4,768]{1,0:T(4,128)S(1)}, f32[4,768,512]{1,2,0:T(8,128)}) fusion(f32[4,768,512]{1,2,0:T(8,128)} %fusion.113, f32[4,768,512]{1,2,0:T(8,128)} %fusion.112, bf16[4,768,1024]{2,1,0:T(8,128)(2,1)} %bitcast.333, bf16[4,512,1024]{2,1,0:T(8,128)(2,1)} %all-gather.11.cloned.1.call-done), kind=kOutput, calls=%fused_computation.17 | convolution fusion | flops 3232232448 | bytes 29372416 | tf_op jit(solution)/shard_map/ead,efd->eaf/dot_general | solution.py:263
  376.3 4.1 all-to-all-start.7
  380.4 9.8 multiply_convert_fusion
  390.2 6.4 fusion.114
  396.6 10.2 %add_convert_fusion = bf16[4,768,1024]{2,1,0:T(8,128)(2,1)S(1)} fusion(f32[4,768,1024]{2,1,0:T(8,128)} %fusion.114, bf16[4,768,512]{1,2,0:T(8,128)(2,1)} %get-tuple-element.84, bf16[4,1024,512]{1,2,0:T(8,128)(2,1)} %all-gather.9.cloned.1.call-done), kind=kOutput, calls=%fused_computation.1 | convolution fusion | flops 3227516928 | bytes 26214400 | tf_op jit(solution)/shard_map/eaf,edf->ead/dot_general | solution.py:276
  407.9 4.5 convolution_convert_fusion.7
  412.4 4.7 all-to-all-start.6
  417.1 12.2 %convolution_convert_fusion.3 = bf16[4,768,1024]{2,1,0:T(8,128)(2,1)} fusion(bf16[4,512,1024]{2,1,0:T(8,128)(2,1)} %all-gather.11.cloned.1.call-done, f32[4,768]{1,0:T(4,128)S(1)} %mul.457, f32[4,768,512]{1,2,0:T(8,128)} %fusion.113, f32[4,768,512]{1,2,0:T(8,128)} %fusion.112), kind=kOutput, calls=%fused_computation.48 | convolution fusion | flops 3235381248 | bytes 23080960 | tf_op jit(solution)/shard_map/eaf,efd->ead/dot_general | solution.py:279
  432.9 4.3 convolution_convert_fusion.8
  437.3 29.0 %all-to-all-done.6 = bf16[8,256,1024]{2,1,0:T(8,128)(2,1)} async-done(((bf16[8,256,1024]{2,1,0:T(8,128)(2,1)}), bf16[8,256,1024]{2,1,0:T(8,128)(2,1)}, u32[]{:S(2)}, u32[]{:S(2)}) %all-to-all-start.6) | async-done | bytes 4194336 | tf_op jit(solution)/shard_map/all_to_all | solution.py:253
  466.2 4.6 all-to-all-start.4
  479.6 40.3 %all-to-all-done.4 = bf16[8,256,1024]{2,1,0:T(8,128)(2,1)} async-done(((bf16[8,256,1024]{2,1,0:T(8,128)(2,1)}), bf16[8,256,1024]{2,1,0:T(8,128)(2,1)}, u32[]{:S(2)}, u32[]{:S(2)}) %all-to-all-start.4) | async-done | bytes 4194336 | tf_op jit(solution)/shard_map/all_to_all | solution.py:253
  529.5 4.1 all-to-all-start.8
  538.0 4.0 concatenate.72
  545.5 5.4 all-to-all-start.12
  553.8 3.8 fusion.9
  563.5 6.6 fusion.3
  589.3 25.5 %all-to-all-done.9 = bf16[4,2,65536]{2,1,0:T(2,128)(2,1)S(1)} async-done(((bf16[4,2,65536]{2,1,0:T(2,128)(2,1)}), bf16[4,2,65536]{2,1,0:T(2,128)(2,1)S(1)}, u32[]{:S(2)}, u32[]{:S(2)}) %all-to-all-start.9) | async-done | bytes 1048608 | tf_op jit(solution)/shard_map/all_to_all | solution.py:369
  618.3 9.9 convolution_convert_fusion.4
  631.5 5.3 all-to-all-start.16
  636.8 7.4 convolution_convert_fusion.5
  646.4 83.4 %all-to-all-done.16 = bf16[4,4,512,256]{3,2,1,0:T(8,128)(2,1)} async-done(((bf16[4,4,512,256]{3,2,1,0:T(8,128)(2,1)}), bf16[4,4,512,256]{3,2,1,0:T(8,128)(2,1)}, u32[]{:S(2)}, u32[]{:S(2)}) %all-to-all-start.16) | async-done | bytes 4194336 | tf_op jit(solution)/shard_map/all_to_all | solution.py:288
  729.8 5.0 all-to-all-start.15
  736.9 3.8 fusion.70
  746.4 81.1 %all-to-all-done.15 = bf16[4,4,256,512]{3,2,1,0:T(8,128)(2,1)} async-done(((bf16[4,4,256,512]{3,2,1,0:T(8,128)(2,1)}), bf16[4,4,256,512]{3,2,1,0:T(8,128)(2,1)}, u32[]{:S(2)}, u32[]{:S(2)}) %all-to-all-start.15) | async-done | bytes 4194336 | tf_op jit(solution)/shard_map/all_to_all | solution.py:288
  827.5 4.8 all-to-all-start.10
  832.3 7.4 convolution_convert_fusion.6
  842.0 42.3 %all-to-all-done.10 = bf16[8,128,2176]{2,1,0:T(8,128)(2,1)} async-done(((bf16[8,128,2176]{2,1,0:T(8,128)(2,1)}), bf16[8,128,2176]{2,1,0:T(8,128)(2,1)}, u32[]{:S(2)}, u32[]{:S(2)}) %all-to-all-start.10) | async-done | bytes 4456480 | tf_op jit(solution)/shard_map/all_to_all | solution.py:298
  884.2 5.0 all-to-all-start.14
  891.3 3.8 reduce_sum.248
  895.1 84.7 %all-to-all-done.14 = bf16[4,4,256,512]{3,2,1,0:T(8,128)(2,1)} async-done(((bf16[4,4,256,512]{3,2,1,0:T(8,128)(2,1)}), bf16[4,4,256,512]{3,2,1,0:T(8,128)(2,1)}, u32[]{:S(2)}, u32[]{:S(2)}) %all-to-all-start.14) | async-done | bytes 4194336 | tf_op jit(solution)/shard_map/all_to_all | solution.py:288
  983.3 4.3 convert_reduce_fusion
  987.6 4.4 convert_reduce_fusion.1
  992.0 4.4 convert_reduce_fusion.2
  (319 shorter events, 153.7 us)
Async XLA Ops:
  7.2 8.6 copy-start.20
  7.2 81.3 %all-gather.5.cloned.1.call-start = ((), (), s32[]{:S(2)}) async-start(), calls=%async_computation.17 | async-start | bytes 7299072 | tf_op jit(solution)/shard_map/all_gather | solution.py:110
  13.4 315.4 %all-gather.9.cloned.1.call-start = ((), (), s32[]{:S(2)}) async-start(), calls=%async_computation.19 | async-start | bytes 5242880 | tf_op jit(solution)/shard_map/all_gather | solution.py:122
  16.6 76.6 %copy-start.64 = (f32[256]{0:T(256)}, f32[256]{0:T(256)S(1)}, u32[]{:S(2)}) copy-start(f32[256]{0:T(256)S(1)} %get-tuple-element.117) | copy-start | bytes 3076
  94.4 6.1 copy-start.59
  94.4 63.8 %copy-start.55 = (s32[1,256,8]{1,2,0:T(8,128)S(1)}, s32[1,256,8]{1,2,0:T(8,128)}, u32[]{:S(2)}) copy-start(s32[1,256,8]{1,2,0:T(8,128)} %param.29) | copy-start | bytes 24580
  95.5 62.7 %all-to-all-start = ((bf16[256,4,512]{0,2,1:T(8,128)(2,1)}), bf16[256,4,512]{0,2,1:T(8,128)(2,1)S(1)}, u32[]{:S(2)}, u32[]{:S(2)}) async-start(bf16[256,4,512]{0,2,1:T(8,128)(2,1)} %pad_maximum_fusion.1), calls=%async_computation | async-start | bytes 2097152 | tf_op jit(solution)/shard_map/all_to_all | solution.py:156
  99.0 239.9 %all-gather.7.cloned.1.call-start = ((), (), s32[]{:S(2)}) async-start(), calls=%async_computation.18 | async-start | bytes 5242880 | tf_op jit(solution)/shard_map/all_gather | solution.py:121
  100.8 67.4 %copy-start.29 = (pred[512,512]{0,1:T(8,128)(4,1)}, pred[512,512]{0,1:T(8,128)(4,1)S(1)}, u32[]{:S(2)}) copy-start(pred[512,512]{0,1:T(8,128)(4,1)S(1)} %fusion.72) | copy-start | bytes 786436
  101.3 73.4 %copy-start.22 = (pred[512,1024]{0,1:T(8,128)(4,1)}, pred[512,1024]{0,1:T(8,128)(4,1)S(1)}, u32[]{:S(2)}) copy-start(pred[512,1024]{0,1:T(8,128)(4,1)S(1)} %fusion.23) | copy-start | bytes 1572868
  158.9 24.7 %all-to-all-start.2 = ((s32[8,8,256]{2,1,0:T(8,128)}), s32[8,8,256]{2,1,0:T(8,128)}, u32[]{:S(2)}, u32[]{:S(2)}) async-start(s32[8,8,256]{2,1,0:T(8,128)} %broadcast_in_dim.99), calls=%async_computation.2 | async-start | bytes 131072 | tf_op jit(solution)/shard_map/all_to_all | solution.py:127
  169.6 10.6 %copy-start.43 = (bf16[512,2,2,64]{0,3,2,1:T(8,128)(2,1)}, bf16[512,2,2,64]{0,3,2,1:T(8,128)(2,1)S(1)}, u32[]{:S(2)}) copy-start(bf16[512,2,2,64]{0,3,2,1:T(8,128)(2,1)S(1)} %fusion.51) | copy-start | bytes 786436
  180.2 6.8 copy-start.18
  183.6 20.9 %all-to-all-start.1 = ((bf16[4,2,32768]{2,1,0:T(2,128)(2,1)}), bf16[4,2,32768]{2,1,0:T(2,128)(2,1)S(1)}, u32[]{:S(2)}, u32[]{:S(2)}) async-start(bf16[4,2,32768]{2,1,0:T(2,128)(2,1)} %reshape.640), calls=%async_computation.1 | async-start | bytes 1048576 | tf_op jit(solution)/shard_map/all_to_all | solution.py:198
  207.0 53.7 %all-to-all-start.5 = ((bf16[8,256,1024]{2,1,0:T(8,128)(2,1)}), bf16[8,256,1024]{2,1,0:T(8,128)(2,1)}, u32[]{:S(2)}, u32[]{:S(2)}) async-start(bf16[8,256,1024]{2,1,0:T(8,128)(2,1)} %broadcast_in_dim.108), calls=%async_computation.5 | async-start | bytes 8388608 | tf_op jit(solution)/shard_map/all_to_all | solution.py:127
  216.3 47.0 %copy-start.10 = (bf16[256,1024]{1,0:T(8,128)(2,1)}, bf16[256,1024]{1,0:T(8,128)(2,1)S(1)}, u32[]{:S(2)}) copy-start(bf16[256,1024]{1,0:T(8,128)(2,1)S(1)} %multiply_convert_fusion.7) | copy-start | bytes 1572868
  263.3 53.7 %all-to-all-start.3 = ((bf16[8,256,1024]{2,1,0:T(8,128)(2,1)}), bf16[8,256,1024]{2,1,0:T(8,128)(2,1)}, u32[]{:S(2)}, u32[]{:S(2)}) async-start(bf16[8,256,1024]{2,1,0:T(8,128)(2,1)} %broadcast_in_dim.101), calls=%async_computation.3 | async-start | bytes 8388608 | tf_op jit(solution)/shard_map/all_to_all | solution.py:127
  267.8 91.7 %all-gather.11.cloned.1.call-start = ((), (), s32[]{:S(2)}) async-start(), calls=%async_computation.20 | async-start | bytes 5242880 | tf_op jit(solution)/shard_map/all_gather | solution.py:123
  270.4 46.5 %copy-start = (pred[8,384,256]{2,1,0:T(32,128)(4,1)}, pred[8,384,256]{2,1,0:T(32,128)(4,1)S(1)}, u32[]{:S(2)}) copy-start(pred[8,384,256]{2,1,0:T(32,128)(4,1)S(1)} %bitcast_compare_fusion) | copy-start | bytes 2359300
  376.3 36.1 %all-to-all-start.7 = ((f32[8,4,256]{2,1,0:T(4,128)}), f32[8,4,256]{2,1,0:T(4,128)S(1)}, u32[]{:S(2)}, u32[]{:S(2)}) async-start(f32[8,4,256]{2,1,0:T(4,128)} %get-tuple-element.82), calls=%async_computation.7 | async-start | bytes 65536 | tf_op jit(solution)/shard_map/all_to_all | solution.py:272
  380.4 9.8 copy-start.13
  390.2 6.4 copy-start.3
  412.4 53.8 %all-to-all-start.6 = ((bf16[8,256,1024]{2,1,0:T(8,128)(2,1)}), bf16[8,256,1024]{2,1,0:T(8,128)(2,1)}, u32[]{:S(2)}, u32[]{:S(2)}) async-start(bf16[8,256,1024]{2,1,0:T(8,128)(2,1)} %convolution_convert_fusion.7), calls=%async_computation.6 | async-start | bytes 8388608 | tf_op jit(solution)/shard_map/all_to_all | solution.py:253
  437.3 33.6 %copy-start.56 = (s32[1,256,8]{1,2,0:T(8,128)S(1)}, s32[1,256,8]{1,2,0:T(8,128)}, u32[]{:S(2)}) copy-start(s32[1,256,8]{1,2,0:T(8,128)} %param.29) | copy-start | bytes 24580
  437.3 33.6 %copy-start.68 = (f32[32]{0:T(128)S(1)}, f32[32]{0:T(128)}, u32[]{:S(2)}) copy-start(f32[32]{0:T(128)} %copy-done.67) | copy-start | bytes 388
  437.3 34.8 %copy-start.11 = (bf16[256,1024]{1,0:T(8,128)(2,1)S(1)}, bf16[256,1024]{1,0:T(8,128)(2,1)}, u32[]{:S(2)}) copy-start(bf16[256,1024]{1,0:T(8,128)(2,1)} %copy-done.10) | copy-start | bytes 1572868
  466.2 53.7 %all-to-all-start.4 = ((bf16[8,256,1024]{2,1,0:T(8,128)(2,1)}), bf16[8,256,1024]{2,1,0:T(8,128)(2,1)}, u32[]{:S(2)}, u32[]{:S(2)}) async-start(bf16[8,256,1024]{2,1,0:T(8,128)(2,1)} %convolution_convert_fusion.8), calls=%async_computation.4 | async-start | bytes 8388608 | tf_op jit(solution)/shard_map/all_to_all | solution.py:253
  476.6 46.5 %copy-start.66 = (f32[256]{0:T(256)S(1)}, f32[256]{0:T(256)}, u32[]{:S(2)}) copy-start(f32[256]{0:T(256)} %get-tuple-element.118) | copy-start | bytes 3076
  525.7 12.3 %copy-start.6 = (f32[256,1024]{1,0:T(8,128)}, f32[256,1024]{1,0:T(8,128)S(1)}, u32[]{:S(2)}) copy-start(f32[256,1024]{1,0:T(8,128)S(1)} %get-tuple-element.92) | copy-start | bytes 3145732
  525.7 7.9 copy-start.52
  525.7 7.9 copy-start.54
  525.7 9.6 copy-start.62
  529.5 16.0 %all-to-all-start.8 = ((bf16[256,4,256]{0,2,1:T(8,128)(2,1)}), bf16[256,4,256]{0,2,1:T(8,128)(2,1)}, u32[]{:S(2)}, u32[]{:S(2)}) async-start(bf16[256,4,256]{0,2,1:T(8,128)(2,1)} %bitcast.67), calls=%async_computation.8 | async-start | bytes 1048576 | tf_op jit(solution)/shard_map/all_to_all | solution.py:328
  542.0 11.1 %copy-start.44 = (bf16[512,2,2,64]{0,3,2,1:T(8,128)(2,1)S(1)}, bf16[512,2,2,64]{0,3,2,1:T(8,128)(2,1)}, u32[]{:S(2)}) copy-start(bf16[512,2,2,64]{0,3,2,1:T(8,128)(2,1)} %copy-done.43) | copy-start | bytes 786436
  542.0 11.8 %copy-start.30 = (pred[512,512]{0,1:T(8,128)(4,1)S(1)}, pred[512,512]{0,1:T(8,128)(4,1)}, u32[]{:S(2)}) copy-start(pred[512,512]{0,1:T(8,128)(4,1)} %copy-done.29) | copy-start | bytes 786436
  545.5 39.1 %all-to-all-start.12 = ((bf16[8,128,1152]{2,1,0:T(8,128)(2,1)}), bf16[8,128,1152]{2,1,0:T(8,128)(2,1)S(1)}, u32[]{:S(2)}, u32[]{:S(2)}) async-start(bf16[8,128,1152]{2,1,0:T(8,128)(2,1)} %concatenate.72), calls=%async_computation.12 | async-start | bytes 4718592 | tf_op jit(solution)/shard_map/all_to_all | solution.py:298
  557.6 5.9 copy-start.23
  563.5 6.6 copy-start.28
  563.5 6.6 copy-start.35
  584.6 30.3 %all-to-all-start.9 = ((bf16[4,2,65536]{2,1,0:T(2,128)(2,1)}), bf16[4,2,65536]{2,1,0:T(2,128)(2,1)S(1)}, u32[]{:S(2)}, u32[]{:S(2)}) async-start(bf16[4,2,65536]{2,1,0:T(2,128)(2,1)} %reshape.642), calls=%async_computation.9 | async-start | bytes 2097152 | tf_op jit(solution)/shard_map/all_to_all | solution.py:369
  614.9 13.4 %copy-start.14 = (bf16[4,2,65536]{2,1,0:T(2,128)(2,1)}, bf16[4,2,65536]{2,1,0:T(2,128)(2,1)S(1)}, u32[]{:S(2)}) copy-start(bf16[4,2,65536]{2,1,0:T(2,128)(2,1)S(1)} %all-to-all-done.9) | copy-start | bytes 3145732
  614.9 15.9 %all-to-all-start.13 = ((bf16[4,32,1152]{2,1,0:T(8,128)(2,1)}), bf16[4,32,1152]{2,1,0:T(8,128)(2,1)S(1)}, u32[]{:S(2)}, u32[]{:S(2)}) async-start(bf16[4,32,1152]{2,1,0:T(8,128)(2,1)} %bitcast.356), calls=%async_computation.13 | async-start | bytes 589824 | tf_op jit(solution)/shard_map/all_to_all | solution.py:306
  631.5 98.4 %all-to-all-start.16 = ((bf16[4,4,512,256]{3,2,1,0:T(8,128)(2,1)}), bf16[4,4,512,256]{3,2,1,0:T(8,128)(2,1)}, u32[]{:S(2)}, u32[]{:S(2)}) async-start(bf16[4,4,512,256]{3,2,1,0:T(8,128)(2,1)} %bitcast.326), calls=%async_computation.16 | async-start | bytes 8388608 | tf_op jit(solution)/shard_map/all_to_all | solution.py:288
  729.8 97.7 %all-to-all-start.15 = ((bf16[4,4,256,512]{3,2,1,0:T(8,128)(2,1)}), bf16[4,4,256,512]{3,2,1,0:T(8,128)(2,1)}, u32[]{:S(2)}, u32[]{:S(2)}) async-start(bf16[4,4,256,512]{3,2,1,0:T(8,128)(2,1)} %bitcast.324), calls=%async_computation.15 | async-start | bytes 8388608 | tf_op jit(solution)/shard_map/all_to_all | solution.py:288
  746.4 85.9 %copy-start.4 = (bf16[4,768,512]{1,2,0:T(8,128)(2,1)S(1)}, bf16[4,768,512]{1,2,0:T(8,128)(2,1)}, u32[]{:S(2)}) copy-start(bf16[4,768,512]{1,2,0:T(8,128)(2,1)} %copy-done.3) | copy-start | bytes 9437188
  827.5 56.7 %all-to-all-start.10 = ((bf16[8,128,2176]{2,1,0:T(8,128)(2,1)}), bf16[8,128,2176]{2,1,0:T(8,128)(2,1)}, u32[]{:S(2)}, u32[]{:S(2)}) async-start(bf16[8,128,2176]{2,1,0:T(8,128)(2,1)} %pad_maximum_fusion), calls=%async_computation.10 | async-start | bytes 8912896 | tf_op jit(solution)/shard_map/all_to_all | solution.py:298
  884.2 95.5 %all-to-all-start.14 = ((bf16[4,4,256,512]{3,2,1,0:T(8,128)(2,1)}), bf16[4,4,256,512]{3,2,1,0:T(8,128)(2,1)}, u32[]{:S(2)}, u32[]{:S(2)}) async-start(bf16[4,4,256,512]{3,2,1,0:T(8,128)(2,1)} %bitcast.325), calls=%async_computation.14 | async-start | bytes 8388608 | tf_op jit(solution)/shard_map/all_to_all | solution.py:288
  979.8 18.2 %all-to-all-start.11 = ((bf16[4,32,2176]{2,1,0:T(8,128)(2,1)}), bf16[4,32,2176]{2,1,0:T(8,128)(2,1)S(1)}, u32[]{:S(2)}, u32[]{:S(2)}) async-start(bf16[4,32,2176]{2,1,0:T(8,128)(2,1)} %bitcast.105), calls=%async_computation.11 | async-start | bytes 1114112 | tf_op jit(solution)/shard_map/all_to_all | solution.py:306
  (44 other events, 119.2 us)
Sparse Core Ops, SparseCore 0:
  13.6 74.8 all-gather.4
  90.6 107.6 all-gather.8
  200.4 78.9 all-gather.6
  280.8 78.7 all-gather.10
